TPU v7x, 32 devices: a whole 2x2x4 slice. The times are simulated.
32 devices in a mesh: dp: 8 (over y, x, core), seq: 4 (over z).
Axes of the slice: x: 2, y: 2, z: 4, core: 2. Of those that a mesh axis runs over, the one named last changes fastest.
Arguments:
- cond_vec: float32 [8, 3072], P('dp', 'seq'), may hold values from -6 to 6
- mod_weight: bfloat16 [2, 3072, 3072], P(None, 'seq', 'dp'), may hold values from -0.109375 to 0.109375
- text_hidden: bfloat16 [8, 512, 3072], P('dp', 'seq'), may hold values from -121 to 121
- text_grad: bfloat16 [8, 512, 3072], P('dp', 'seq'), may hold values from -14 to 14, as said below
- queries: bfloat16 [8, 2048, 2048], P('dp', 'seq'), may hold values from -4.5 to 4.5
- keys: bfloat16 [8, 2048, 2048], P('dp', 'seq'), may hold values from -4.5 to 4.5
- values: bfloat16 [8, 2048, 2048], P('dp', 'seq'), may hold values from -6 to 6
- out_grad: bfloat16 [8, 2048, 2048], P('dp', 'seq'), may hold values from -6 to 6
Outputs:
- text_hidden_grad: bfloat16 [8, 512, 3072], P('dp', 'seq')
- mod_weight_grad: float32 [2, 3072, 3072], P(None, 'seq', 'dp')
- cond_vec_grad: float32 [8, 3072], P('dp', 'seq')
- query_grad: bfloat16 [8, 2048, 2048], P('dp', 'seq')
- key_grad: bfloat16 [8, 2048, 2048], P('dp', 'seq')
- value_grad: bfloat16 [8, 2048, 2048], P('dp', 'seq')
Inputs may be any that keep to these rules, and one draw needn't show every extreme that they name: `text_grad`: incoming gradient.
All inputs are finite; a program needn't handle non-finite values.
Results may differ from a plain program's by a relative error of at most 0.0087.
Values may be sent and summed in bfloat16 or wider, within the bound.
No kernel may reach another device: no remote copies, remote signals or barrier semaphores. Data moves between devices by JAX's collectives and lax.ppermute only.
A program may use at most 128 MiB of HBM per device.

v0:
```python
import functools
import math

import jax
import jax.numpy as jnp
from jax import lax
from jax.experimental import pallas as pl
from jax.experimental.pallas import tpu as pltpu
from jax.sharding import PartitionSpec as P

HEADS = 16
HEAD_DIM = 128
VMEM_BYTES = 60 * 1024 * 1024
norm_eps = 1e-06


def fold_rows(array, combine):
    rows, lanes = array.shape
    return combine(array.reshape(rows // 8, 8, lanes), axis=0)


def attend_kernel(parts, rows, width, query_block, key_block, *refs):
    ins, outs = refs[:parts], refs[parts : 2 * parts]
    (q_all, k_all, v_all, g_all, k_flip, q_flip, g_flip, score, prob_grad, key_sum, value_sum,
     query_flip, query_out) = refs[2 * parts :]
    total = parts * rows
    factor = width ** (-0.5)
    scale = factor * math.log2(math.e)
    for part in range(parts):
        here = slice(part * rows, (part + 1) * rows)
        q_all[here, :] = ins[part][0]
        k_all[here, :] = ins[part][1]
        v_all[here, :] = ins[part][2]
        g_all[here, :] = ins[part][3]
        k_flip[:, here] = ins[part][1].T
    key_sum[...] = jnp.zeros_like(key_sum)
    value_sum[...] = jnp.zeros_like(value_sum)

    def one_block(index, _):
        mine = pl.ds(pl.multiple_of(index * query_block, query_block), query_block)
        q_flip[...] = q_all[mine, :].T
        g_flip[...] = g_all[mine, :].T

        def first(step, peak):
            at = pl.ds(pl.multiple_of(step * key_block, key_block), key_block)
            part_score = jnp.dot(k_all[at, :], q_flip[...], preferred_element_type=jnp.float32)
            score[at, :] = part_score
            prob_grad[at, :] = jnp.dot(
                v_all[at, :], g_flip[...], preferred_element_type=jnp.float32
            )
            return jnp.maximum(peak, fold_rows(part_score, jnp.max))

        peak = lax.fori_loop(
            0, total // key_block, first, jnp.full((8, query_block), -jnp.inf, jnp.float32)
        )
        peak = jnp.max(peak, axis=0, keepdims=True)

        def second(step, carry):
            sums, deltas = carry
            at = pl.ds(pl.multiple_of(step * key_block, key_block), key_block)
            exponent = jnp.exp2((score[at, :] - peak) * scale)
            score[at, :] = exponent
            sums = sums + fold_rows(exponent, jnp.sum)
            deltas = deltas + fold_rows(exponent * prob_grad[at, :], jnp.sum)
            return sums, deltas

        empty = jnp.zeros((8, query_block), jnp.float32)
        sums, deltas = lax.fori_loop(0, total // key_block, second, (empty, empty))
        inverse = 1.0 / jnp.sum(sums, axis=0, keepdims=True)
        delta = jnp.sum(deltas, axis=0, keepdims=True) * inverse
        query_flip[...] = jnp.zeros_like(query_flip)

        def third(step, _):
            at = pl.ds(pl.multiple_of(step * key_block, key_block), key_block)
            probability = score[at, :] * inverse
            prob_low = probability.astype(jnp.bfloat16)
            score_low = (probability * (prob_grad[at, :] - delta)).astype(jnp.bfloat16)
            value_sum[at, :] += jnp.dot(
                prob_low, g_all[mine, :], preferred_element_type=jnp.float32
            )
            key_sum[at, :] += jnp.dot(score_low, q_all[mine, :], preferred_element_type=jnp.float32)
            query_flip[...] += jnp.dot(
                k_flip[:, at], score_low, preferred_element_type=jnp.float32
            )
            return 0

        lax.fori_loop(0, total // key_block, third, 0)
        query_out[mine, :] = (query_flip[...] * factor).T.astype(jnp.bfloat16)
        return 0

    lax.fori_loop(0, total // query_block, one_block, 0)
    for part in range(parts):
        here = slice(part * rows, (part + 1) * rows)
        outs[part][0] = query_out[here, :]
        outs[part][1] = (key_sum[here, :] * factor).astype(jnp.bfloat16)
        outs[part][2] = value_sum[here, :].astype(jnp.bfloat16)


def attend(pieces):
    parts = len(pieces)
    _, rows, width = pieces[0].shape
    total = parts * rows
    query_block = math.gcd(total, 512)
    key_block = math.gcd(total, 512)
    low, wide = jnp.bfloat16, jnp.float32
    pairs = total * total
    return pl.pallas_call(
        functools.partial(attend_kernel, parts, rows, width, query_block, key_block),
        out_shape=[jax.ShapeDtypeStruct((3, rows, width), low)] * parts,
        in_specs=[pl.BlockSpec(memory_space=pltpu.VMEM)] * parts,
        out_specs=[pl.BlockSpec(memory_space=pltpu.VMEM)] * parts,
        scratch_shapes=[
            pltpu.VMEM((total, width), low),
            pltpu.VMEM((total, width), low),
            pltpu.VMEM((total, width), low),
            pltpu.VMEM((total, width), low),
            pltpu.VMEM((width, total), low),
            pltpu.VMEM((width, query_block), low),
            pltpu.VMEM((width, query_block), low),
            pltpu.VMEM((total, query_block), wide),
            pltpu.VMEM((total, query_block), wide),
            pltpu.VMEM((total, width), wide),
            pltpu.VMEM((total, width), wide),
            pltpu.VMEM((width, query_block), wide),
            pltpu.VMEM((total, width), low),
        ],
        cost_estimate=pl.CostEstimate(
            flops=10 * pairs * width,
            bytes_accessed=7 * total * width * 2,
            transcendentals=pairs,
        ),
        compiler_params=pltpu.CompilerParams(vmem_limit_bytes=VMEM_BYTES),
        name="attend",
    )(*pieces)


def pack_kernel(parts, *refs):
    ins, outs = refs[1 : 1 + 4 * parts], refs[1 + 4 * parts :]
    for part in range(parts):
        for which in range(4):
            outs[part][which] = ins[4 * part + which][...]


def pack(place, arrays, parts, per_device, local):
    rows = arrays[0].shape[0]

    def spec_for(offset):
        return pl.BlockSpec(
            (rows, HEAD_DIM),
            lambda step, at: (0, lax.rem(at[0] + offset, parts) * per_device + local),
        )

    specs = [spec_for(offset) for offset in range(parts) for _ in range(4)]
    shape = (4, rows, HEAD_DIM)
    return pl.pallas_call(
        functools.partial(pack_kernel, parts),
        out_shape=[jax.ShapeDtypeStruct(shape, jnp.bfloat16)] * parts,
        grid_spec=pltpu.PrefetchScalarGridSpec(
            num_scalar_prefetch=1,
            grid=(1,),
            in_specs=specs,
            out_specs=[pl.BlockSpec(shape, lambda step, at: (0, 0, 0))] * parts,
        ),
        cost_estimate=pl.CostEstimate(
            flops=0, bytes_accessed=2 * parts * 4 * rows * HEAD_DIM * 2, transcendentals=0
        ),
        compiler_params=pltpu.CompilerParams(vmem_limit_bytes=VMEM_BYTES),
        name="pack",
    )(place, *(list(arrays) * parts))


def unpack_kernel(parts, *refs):
    ins, outs = refs[1 : 1 + parts], refs[-3:]
    step = pl.program_id(0)
    for part in range(parts):

        @pl.when(step == part)
        def _():
            for which in range(3):
                outs[which][...] = ins[part][which]


def unpack(place, pieces, joined, per_device, local):
    parts = len(pieces)
    _, rows, width = pieces[0].shape
    shape = (3, rows, width)
    out_spec = pl.BlockSpec(
        (rows, width), lambda step, at: (0, lax.rem(at[0] + step, parts) * per_device + local)
    )
    specs = [pl.BlockSpec(shape, lambda step, at: (0, 0, 0))] * parts
    previous = [] if joined is None else list(joined)
    specs += [pl.BlockSpec(memory_space=pl.ANY)] * len(previous)
    return pl.pallas_call(
        functools.partial(unpack_kernel, parts),
        out_shape=[jax.ShapeDtypeStruct((rows, parts * per_device * width), jnp.bfloat16)] * 3,
        grid_spec=pltpu.PrefetchScalarGridSpec(
            num_scalar_prefetch=1, grid=(parts,), in_specs=specs, out_specs=[out_spec] * 3
        ),
        input_output_aliases={1 + parts + which: which for which in range(len(previous))},
        cost_estimate=pl.CostEstimate(
            flops=0, bytes_accessed=2 * parts * 3 * rows * width * 2, transcendentals=0
        ),
        compiler_params=pltpu.CompilerParams(vmem_limit_bytes=VMEM_BYTES),
        name="unpack",
    )(place, *pieces, *previous)


def per_device(cond_vec, mod_weight, text_hidden, text_grad, queries, keys, values, out_grad):
    parts = lax.axis_size("seq")
    samples = queries.shape[0]
    heads_here = HEADS // parts
    place = lax.axis_index("seq")
    place_array = jnp.reshape(place, (1,)).astype(jnp.int32)

    def shift(array, offset):
        ring = [(index, (index + offset) % parts) for index in range(parts)]
        return lax.ppermute(array, "seq", ring)

    order = sorted(range(1, parts), key=lambda offset: -min(offset, parts - offset))

    hidden = text_hidden.astype(jnp.float32)
    incoming = text_grad.astype(jnp.float32)
    centred = hidden - jnp.mean(hidden, axis=-1, keepdims=True)
    inv_std = lax.rsqrt(jnp.mean(centred * centred, axis=-1, keepdims=True) + norm_eps)
    normed = centred * inv_std
    grad_mod = jnp.stack([jnp.sum(incoming, axis=1), jnp.sum(incoming * normed, axis=1)], axis=1)
    grad_parts = [grad_mod] + [shift(grad_mod, offset) for offset in order]

    cond_all = lax.all_gather(cond_vec, "dp", axis=0, tiled=True)
    act = jax.nn.silu(cond_all).astype(jnp.bfloat16)
    partial_scale = jnp.dot(act, mod_weight[1], preferred_element_type=jnp.float32)
    own_scale = lax.all_to_all(partial_scale, "dp", split_axis=0, concat_axis=1, tiled=True)
    scale_parts = [own_scale] + [shift(own_scale, offset) for offset in order]

    work = [(sample, local) for sample in range(samples) for local in range(heads_here)]
    arrived = []
    for sample, local in work:
        arrays = [array[sample] for array in (queries, keys, values, out_grad)]
        packed = pack(place_array, arrays, parts, heads_here, local)
        pieces = {offset: shift(packed[offset], offset) for offset in order}
        arrived.append([packed[0]] + [pieces[offset] for offset in range(1, parts)])
    back = []
    for index in range(len(work)):
        grads = attend(arrived[index])
        pieces = {offset: shift(grads[offset], parts - offset) for offset in order}
        back.append([grads[0]] + [pieces[offset] for offset in range(1, parts)])

    def after(arrays, index):
        if index >= len(back):
            return arrays
        arrays, back[index][0] = lax.optimization_barrier((arrays, back[index][0]))
        return arrays

    grad_parts = after(grad_parts, 0)
    scale_parts = after(scale_parts, 1)
    summed_grad = sum(grad_parts)
    owner_grad = lax.all_to_all(summed_grad, "dp", split_axis=2, concat_axis=0, tiled=True)
    mod_scale = sum(scale_parts)
    text_hidden, text_grad = after((text_hidden, text_grad), 1)
    hidden = text_hidden.astype(jnp.float32)
    incoming = text_grad.astype(jnp.float32)
    centred = hidden - jnp.mean(hidden, axis=-1, keepdims=True)
    inv_std = lax.rsqrt(jnp.mean(centred * centred, axis=-1, keepdims=True) + norm_eps)
    normed = centred * inv_std
    upstream = incoming * (1.0 + mod_scale[:, None, :])
    text_hidden_grad = inv_std * (
        upstream
        - jnp.mean(upstream, axis=-1, keepdims=True)
        - normed * jnp.mean(upstream * normed, axis=-1, keepdims=True)
    )
    text_hidden_grad = text_hidden_grad.astype(jnp.bfloat16)
    mod_weight_grad = jnp.einsum(
        "br,bkc->krc", act.astype(jnp.float32), owner_grad, precision=lax.Precision.HIGHEST
    )
    backward = jnp.einsum(
        "bkc,krc->br", owner_grad, mod_weight.astype(jnp.float32), precision=lax.Precision.HIGHEST
    )
    summed_back = lax.psum_scatter(backward, "dp", scatter_dimension=0, tiled=True)
    sigma = jax.nn.sigmoid(cond_vec)
    cond_vec_grad = summed_back * sigma * (1.0 + cond_vec * (1.0 - sigma))

    joined = [None] * samples
    for index, (sample, local) in enumerate(work):
        joined[sample] = unpack(place_array, back[index], joined[sample], heads_here, local)
    query_grad, key_grad, value_grad = (
        jnp.stack([joined[sample][which] for sample in range(samples)]) for which in range(3)
    )
    return (text_hidden_grad, mod_weight_grad, cond_vec_grad, query_grad, key_grad, value_grad)


def solution(mesh):
    return jax.shard_map(
        per_device,
        mesh=mesh,
        in_specs=(
            P("dp", "seq"),
            P(None, "seq", "dp"),
            P("dp", "seq", None),
            P("dp", "seq", None),
            P("dp", "seq", None),
            P("dp", "seq", None),
            P("dp", "seq", None),
            P("dp", "seq", None),
        ),
        out_specs=(
            P("dp", "seq", None),
            P(None, "seq", "dp"),
            P("dp", "seq"),
            P("dp", "seq", None),
            P("dp", "seq", None),
            P("dp", "seq", None),
        ),
        check_vma=False,
    )
```

profile of v0, /device:TPU:0, one launch (start us, length us, event | category | flops | bytes accessed | tf_op | source)
XLA Modules:
  0.0 370.5 jit_solution(11671624286975396849)
XLA Ops:
  3.7 4.1 %collective-permute-start.10 = (bf16[4,512,128]{2,1,0:T(8,128)(2,1)}, bf16[4,512,128]{2,1,0:T(8,128)(2,1)}, u32[]{:S(2)}, u32[]{:S(2)}) collective-permute-start(bf16[4,512,128]{2,1,0:T(8,128)(2,1)} %get-tuple-element.77), channel_id=1, source_target_pairs={{0,2},{1,3},{2,0},{3,1},{4,6},{5,7},{6,4},{7,5},{8,10},{9,11},{10,... | collective-permute-start | bytes 1572872 | tf_op jit(solution)/shard_map/ppermute | solution.py:217
  16.5 9.1 %all-gather = f32[8,1,768]{2,1,0:T(1,128)S(1)} all-gather(f32[1,1,768]{2,1,0:T(1,128)S(1)} %bitcast.131), channel_id=1, replica_groups=mesh['dp'=8,'seq'=4] {'dp'}, dimensions={0}, use_global_device_ids=true | all-gather | bytes 27648 | tf_op jit(solution)/shard_map/all_gather | solution.py:229
  26.8 3.3 all-to-all-start
  33.0 13.2 %collective-permute-start.5 = (bf16[4,512,128]{2,1,0:T(8,128)(2,1)S(1)}, bf16[4,512,128]{2,1,0:T(8,128)(2,1)S(1)}, u32[]{:S(2)}, u32[]{:S(2)}) collective-permute-start(bf16[4,512,128]{2,1,0:T(8,128)(2,1)S(1)} %copy-done.16), channel_id=1, source_target_pairs={{0,3},{1,0},{2,1},{3,2},{4,7},{5,4},{6,5},{7,6},{8,11},{9,8},{10,9... | collective-permute-start | bytes 1572872 | tf_op jit(solution)/shard_map/ppermute | solution.py:217
  46.1 3.0 pack.7
  52.8 23.7 %collective-permute-start.6 = (f32[1,2,3072]{2,1,0:T(2,128)S(1)}, f32[1,2,3072]{2,1,0:T(2,128)S(1)}, u32[]{:S(2)}, u32[]{:S(2)}) collective-permute-start(f32[1,2,3072]{2,1,0:T(2,128)S(1)} %pad_maximum_fusion), channel_id=1, source_target_pairs={{0,2},{1,3},{2,0},{3,1},{4,6},{5,7},{6,4},{7,5},{8,10},{9,11},{10,... | collective-permute-start | bytes 73736 | tf_op jit(solution)/shard_map/ppermute | solution.py:217
  77.6 22.5 %attend.5 = (bf16[3,512,128]{2,1,0:T(8,128)(2,1)}, bf16[3,512,128]{2,1,0:T(8,128)(2,1)}, bf16[3,512,128]{2,1,0:T(8,128)(2,1)}, bf16[3,512,128]{2,1,0:T(8,128)(2,1)}) custom-call(bf16[4,512,128]{2,1,0:T(8,128)(2,1)} %get-tuple-element.75.refs_0_, bf16[4,512,128]{2,1,0:T(8,128)(2,1)} %collective-permute-done.9.refs_1_, ...), custom_call_target="tpu_custom_call" | custom-call | flops 5368709120 | bytes 3670016 | tf_op jit(solution)/shard_map/attend/pallas_call | solution.py:107
  100.1 3.1 collective-permute-start.8
  107.1 22.7 %attend.4 = (bf16[3,512,128]{2,1,0:T(8,128)(2,1)}, bf16[3,512,128]{2,1,0:T(8,128)(2,1)}, bf16[3,512,128]{2,1,0:T(8,128)(2,1)}, bf16[3,512,128]{2,1,0:T(8,128)(2,1)}) custom-call(bf16[4,512,128]{2,1,0:T(8,128)(2,1)} %get-tuple-element.63.refs_0_, bf16[4,512,128]{2,1,0:T(8,128)(2,1)} %collective-permute-done.3.refs_1_, ...), custom_call_target="tpu_custom_call" | custom-call | flops 5368709120 | bytes 3670016 | tf_op jit(solution)/shard_map/attend/pallas_call | solution.py:107
  137.9 14.8 %reduce.8 = f32[3072,2]{1,0:T(8,128)} reduce(f32[3072,1,2]{2,1,0:T(1,128)S(1)} %bitcast.122, f32[]{:T(128)} %broadcast.83), dimensions={1}, to_apply=%bitcast.51.reduce_sub_computation | reduce | bytes 49156
  152.7 3.0 reshape.104
  155.8 3.8 %all-to-all-start.1 = ((f32[8,1,768]{2,1,0:T(1,128)}), f32[8,1,768]{2,1,0:T(1,128)S(1)}, u32[]{:S(2)}, u32[]{:S(2)}) async-start(f32[8,1,768]{2,1,0:T(1,128)} %reshape.104), calls=%async_computation.1 | async-start | bytes 49152 | tf_op jit(solution)/shard_map/all_to_all | solution.py:257
  165.1 4.2 %collective-permute-done.19.refs_2_ = bf16[4,512,128]{2,1,0:T(8,128)(2,1)} collective-permute-done((bf16[4,512,128]{2,1,0:T(8,128)(2,1)}, bf16[4,512,128]{2,1,0:T(8,128)(2,1)}, u32[]{:S(2)}, u32[]{:S(2)}) %collective-permute-start.19) | collective-permute-done | bytes 524320 | tf_op jit(solution)/shard_map/ppermute | solution.py:217
  169.3 42.1 %collective-permute-start.27 = (bf16[3,512,128]{2,1,0:T(8,128)(2,1)}, bf16[3,512,128]{2,1,0:T(8,128)(2,1)S(1)}, u32[]{:S(2)}, u32[]{:S(2)}) collective-permute-start(bf16[3,512,128]{2,1,0:T(8,128)(2,1)} %get-tuple-element.105), channel_id=1, source_target_pairs={{0,3},{1,0},{2,1},{3,2},{4,7},{5,4},{6,5},{7,6},{8,11},{9,8},{10,9... | collective-permute-start | bytes 1179656 | tf_op jit(solution)/shard_map/ppermute | solution.py:217
  211.4 22.6 %attend.7 = (bf16[3,512,128]{2,1,0:T(8,128)(2,1)}, bf16[3,512,128]{2,1,0:T(8,128)(2,1)}, bf16[3,512,128]{2,1,0:T(8,128)(2,1)}, bf16[3,512,128]{2,1,0:T(8,128)(2,1)}) custom-call(bf16[4,512,128]{2,1,0:T(8,128)(2,1)} %get-tuple-element.92.refs_0_, bf16[4,512,128]{2,1,0:T(8,128)(2,1)} %collective-permute-done.18.refs_1_, ...), custom_call_target="tpu_custom_call" | custom-call | flops 5368709120 | bytes 3670016 | tf_op jit(solution)/shard_map/attend/pallas_call | solution.py:107
  234.7 7.8 %collective-permute-start.24 = (bf16[3,512,128]{2,1,0:T(8,128)(2,1)}, bf16[3,512,128]{2,1,0:T(8,128)(2,1)S(1)}, u32[]{:S(2)}, u32[]{:S(2)}) collective-permute-start(bf16[3,512,128]{2,1,0:T(8,128)(2,1)} %get-tuple-element.101), channel_id=1, source_target_pairs={{0,3},{1,0},{2,1},{3,2},{4,7},{5,4},{6,5},{7,6},{8,11},{9,8},{10,9... | collective-permute-start | bytes 1179656 | tf_op jit(solution)/shard_map/ppermute | solution.py:217
  242.5 8.1 %collective-permute-start.26 = (bf16[3,512,128]{2,1,0:T(8,128)(2,1)}, bf16[3,512,128]{2,1,0:T(8,128)(2,1)}, u32[]{:S(2)}, u32[]{:S(2)}) collective-permute-start(bf16[3,512,128]{2,1,0:T(8,128)(2,1)} %get-tuple-element.103), channel_id=1, source_target_pairs={{0,1},{1,2},{2,3},{3,0},{4,5},{5,6},{6,7},{7,4},{8,9},{9,10},{10,1... | collective-permute-start | bytes 1179656 | tf_op jit(solution)/shard_map/ppermute | solution.py:217
  250.6 23.5 %collective-permute-done.28.refs_3_ = bf16[3,512,128]{2,1,0:T(8,128)(2,1)S(1)} collective-permute-done((bf16[3,512,128]{2,1,0:T(8,128)(2,1)S(1)}, bf16[3,512,128]{2,1,0:T(8,128)(2,1)S(1)}, u32[]{:S(2)}, u32[]{:S(2)}) %collective-permute-start.28) | collective-permute-done | bytes 393248 | tf_op jit(solution)/shard_map/ppermute | solution.py:217
  274.9 22.7 %attend.6 = (bf16[3,512,128]{2,1,0:T(8,128)(2,1)}, bf16[3,512,128]{2,1,0:T(8,128)(2,1)}, bf16[3,512,128]{2,1,0:T(8,128)(2,1)}, bf16[3,512,128]{2,1,0:T(8,128)(2,1)}) custom-call(bf16[4,512,128]{2,1,0:T(8,128)(2,1)} %get-tuple-element.84.refs_0_, bf16[4,512,128]{2,1,0:T(8,128)(2,1)} %collective-permute-done.12.refs_1_, ...), custom_call_target="tpu_custom_call" | custom-call | flops 5368709120 | bytes 3670016 | tf_op jit(solution)/shard_map/attend/pallas_call | solution.py:107
  314.9 23.3 %all-reduce = f32[8,768]{1,0:T(8,128)S(1)} all-reduce(f32[8,768]{1,0:T(8,128)S(1)} %convolution_bitcast_fusion.1), channel_id=2, replica_groups=mesh['dp'=8,'seq'=4] {'dp'}, use_global_device_ids=true, to_apply=%region_8.9.clone | all-reduce | flops 6144 | bytes 49152
  339.4 3.0 unpack.4
  342.5 3.1 unpack.5
  349.5 17.0 %collective-permute-done.16.refs_3_ = bf16[3,512,128]{2,1,0:T(8,128)(2,1)S(1)} collective-permute-done((bf16[3,512,128]{2,1,0:T(8,128)(2,1)}, bf16[3,512,128]{2,1,0:T(8,128)(2,1)S(1)}, u32[]{:S(2)}, u32[]{:S(2)}) %collective-permute-start.16) | collective-permute-done | bytes 393248 | tf_op jit(solution)/shard_map/ppermute | solution.py:217
  367.5 3.0 unpack.7
  (125 shorter events, 62.8 us)
Async XLA Ops:
  7.7 45.1 %collective-permute-start.11 = (bf16[4,512,128]{2,1,0:T(8,128)(2,1)}, bf16[4,512,128]{2,1,0:T(8,128)(2,1)}, u32[]{:S(2)}, u32[]{:S(2)}) collective-permute-start(bf16[4,512,128]{2,1,0:T(8,128)(2,1)} %get-tuple-element.78), channel_id=1, source_target_pairs={{0,3},{1,0},{2,1},{3,2},{4,7},{5,4},{6,5},{7,6},{8,11},{9,8},{10,9... | collective-permute-start | bytes 1572872 | tf_op jit(solution)/shard_map/ppermute | solution.py:217
  9.1 67.5 %collective-permute-start.9 = (bf16[4,512,128]{2,1,0:T(8,128)(2,1)}, bf16[4,512,128]{2,1,0:T(8,128)(2,1)}, u32[]{:S(2)}, u32[]{:S(2)}) collective-permute-start(bf16[4,512,128]{2,1,0:T(8,128)(2,1)} %get-tuple-element.76), channel_id=1, source_target_pairs={{0,1},{1,2},{2,3},{3,0},{4,5},{5,6},{6,7},{7,4},{8,9},{9,10},{10,1... | collective-permute-start | bytes 1572872 | tf_op jit(solution)/shard_map/ppermute | solution.py:217
  12.8 90.5 %collective-permute-start.3 = (bf16[4,512,128]{2,1,0:T(8,128)(2,1)}, bf16[4,512,128]{2,1,0:T(8,128)(2,1)}, u32[]{:S(2)}, u32[]{:S(2)}) collective-permute-start(bf16[4,512,128]{2,1,0:T(8,128)(2,1)} %get-tuple-element.64), channel_id=1, source_target_pairs={{0,1},{1,2},{2,3},{3,0},{4,5},{5,6},{6,7},{7,4},{8,9},{9,10},{10,1... | collective-permute-start | bytes 1572872 | tf_op jit(solution)/shard_map/ppermute | solution.py:217
  14.4 88.9 %collective-permute-start.4 = (bf16[4,512,128]{2,1,0:T(8,128)(2,1)}, bf16[4,512,128]{2,1,0:T(8,128)(2,1)}, u32[]{:S(2)}, u32[]{:S(2)}) collective-permute-start(bf16[4,512,128]{2,1,0:T(8,128)(2,1)} %get-tuple-element.65), channel_id=1, source_target_pairs={{0,2},{1,3},{2,0},{3,1},{4,6},{5,7},{6,4},{7,5},{8,10},{9,11},{10,... | collective-permute-start | bytes 1572872 | tf_op jit(solution)/shard_map/ppermute | solution.py:217
  26.8 76.4 %all-to-all-start = ((f32[8,1,384]{2,1,0:T(1,128)}), f32[8,1,384]{2,1,0:T(1,128)S(1)}, u32[]{:S(2)}, u32[]{:S(2)}) async-start(f32[8,1,384]{2,1,0:T(1,128)} %copy.27), calls=%async_computation | async-start | bytes 24576 | tf_op jit(solution)/shard_map/all_to_all | solution.py:232
  33.0 72.1 %collective-permute-start.5 = (bf16[4,512,128]{2,1,0:T(8,128)(2,1)S(1)}, bf16[4,512,128]{2,1,0:T(8,128)(2,1)S(1)}, u32[]{:S(2)}, u32[]{:S(2)}) collective-permute-start(bf16[4,512,128]{2,1,0:T(8,128)(2,1)S(1)} %copy-done.16), channel_id=1, source_target_pairs={{0,3},{1,0},{2,1},{3,2},{4,7},{5,4},{6,5},{7,6},{8,11},{9,8},{10,9... | collective-permute-start | bytes 1572872 | tf_op jit(solution)/shard_map/ppermute | solution.py:217
  52.8 47.3 %collective-permute-start.6 = (f32[1,2,3072]{2,1,0:T(2,128)S(1)}, f32[1,2,3072]{2,1,0:T(2,128)S(1)}, u32[]{:S(2)}, u32[]{:S(2)}) collective-permute-start(f32[1,2,3072]{2,1,0:T(2,128)S(1)} %pad_maximum_fusion), channel_id=1, source_target_pairs={{0,2},{1,3},{2,0},{3,1},{4,6},{5,7},{6,4},{7,5},{8,10},{9,11},{10,... | collective-permute-start | bytes 73736 | tf_op jit(solution)/shard_map/ppermute | solution.py:217
  76.6 53.2 %collective-permute-start.7 = (f32[1,2,3072]{2,1,0:T(2,128)S(1)}, f32[1,2,3072]{2,1,0:T(2,128)S(1)}, u32[]{:S(2)}, u32[]{:S(2)}) collective-permute-start(f32[1,2,3072]{2,1,0:T(2,128)S(1)} %pad_maximum_fusion), channel_id=1, source_target_pairs={{0,1},{1,2},{2,3},{3,0},{4,5},{5,6},{6,7},{7,4},{8,9},{9,10},{10,1... | collective-permute-start | bytes 73736 | tf_op jit(solution)/shard_map/ppermute | solution.py:217
  131.1 80.4 %collective-permute-start.20 = (bf16[4,512,128]{2,1,0:T(8,128)(2,1)}, bf16[4,512,128]{2,1,0:T(8,128)(2,1)}, u32[]{:S(2)}, u32[]{:S(2)}) collective-permute-start(bf16[4,512,128]{2,1,0:T(8,128)(2,1)} %get-tuple-element.95), channel_id=1, source_target_pairs={{0,3},{1,0},{2,1},{3,2},{4,7},{5,4},{6,5},{7,6},{8,11},{9,8},{10,9... | collective-permute-start | bytes 1572872 | tf_op jit(solution)/shard_map/ppermute | solution.py:217
  133.7 100.3 %collective-permute-start.12 = (bf16[4,512,128]{2,1,0:T(8,128)(2,1)}, bf16[4,512,128]{2,1,0:T(8,128)(2,1)}, u32[]{:S(2)}, u32[]{:S(2)}) collective-permute-start(bf16[4,512,128]{2,1,0:T(8,128)(2,1)} %get-tuple-element.85), channel_id=1, source_target_pairs={{0,1},{1,2},{2,3},{3,0},{4,5},{5,6},{6,7},{7,4},{8,9},{9,10},{10,1... | collective-permute-start | bytes 1572872 | tf_op jit(solution)/shard_map/ppermute | solution.py:217
  134.5 100.2 %collective-permute-start.13 = (bf16[4,512,128]{2,1,0:T(8,128)(2,1)}, bf16[4,512,128]{2,1,0:T(8,128)(2,1)}, u32[]{:S(2)}, u32[]{:S(2)}) collective-permute-start(bf16[4,512,128]{2,1,0:T(8,128)(2,1)} %get-tuple-element.86), channel_id=1, source_target_pairs={{0,2},{1,3},{2,0},{3,1},{4,6},{5,7},{6,4},{7,5},{8,10},{9,11},{10,... | collective-permute-start | bytes 1572872 | tf_op jit(solution)/shard_map/ppermute | solution.py:217
  155.8 141.8 %all-to-all-start.1 = ((f32[8,1,768]{2,1,0:T(1,128)}), f32[8,1,768]{2,1,0:T(1,128)S(1)}, u32[]{:S(2)}, u32[]{:S(2)}) async-start(f32[8,1,768]{2,1,0:T(1,128)} %reshape.104), calls=%async_computation.1 | async-start | bytes 49152 | tf_op jit(solution)/shard_map/all_to_all | solution.py:257
  160.7 81.7 %collective-permute-start.14 = (bf16[4,512,128]{2,1,0:T(8,128)(2,1)S(1)}, bf16[4,512,128]{2,1,0:T(8,128)(2,1)S(1)}, u32[]{:S(2)}, u32[]{:S(2)}) collective-permute-start(bf16[4,512,128]{2,1,0:T(8,128)(2,1)S(1)} %copy-done.15), channel_id=1, source_target_pairs={{0,3},{1,0},{2,1},{3,2},{4,7},{5,4},{6,5},{7,6},{8,11},{9,8},{10,9... | collective-permute-start | bytes 1572872 | tf_op jit(solution)/shard_map/ppermute | solution.py:217
  169.3 73.1 %collective-permute-start.27 = (bf16[3,512,128]{2,1,0:T(8,128)(2,1)}, bf16[3,512,128]{2,1,0:T(8,128)(2,1)S(1)}, u32[]{:S(2)}, u32[]{:S(2)}) collective-permute-start(bf16[3,512,128]{2,1,0:T(8,128)(2,1)} %get-tuple-element.105), channel_id=1, source_target_pairs={{0,3},{1,0},{2,1},{3,2},{4,7},{5,4},{6,5},{7,6},{8,11},{9,8},{10,9... | collective-permute-start | bytes 1179656 | tf_op jit(solution)/shard_map/ppermute | solution.py:217
  211.4 62.7 %collective-permute-start.28 = (bf16[3,512,128]{2,1,0:T(8,128)(2,1)S(1)}, bf16[3,512,128]{2,1,0:T(8,128)(2,1)S(1)}, u32[]{:S(2)}, u32[]{:S(2)}) collective-permute-start(bf16[3,512,128]{2,1,0:T(8,128)(2,1)S(1)} %copy-done.19), channel_id=1, source_target_pairs={{0,2},{1,3},{2,0},{3,1},{4,6},{5,7},{6,4},{7,5},{8,10},{9,11},{10,... | collective-permute-start | bytes 1179656 | tf_op jit(solution)/shard_map/ppermute | solution.py:217
  234.0 71.7 %collective-permute-start.29 = (bf16[3,512,128]{2,1,0:T(8,128)(2,1)}, bf16[3,512,128]{2,1,0:T(8,128)(2,1)}, u32[]{:S(2)}, u32[]{:S(2)}) collective-permute-start(bf16[3,512,128]{2,1,0:T(8,128)(2,1)} %get-tuple-element.107), channel_id=1, source_target_pairs={{0,1},{1,2},{2,3},{3,0},{4,5},{5,6},{6,7},{7,4},{8,9},{9,10},{10,1... | collective-permute-start | bytes 1179656 | tf_op jit(solution)/shard_map/ppermute | solution.py:217
  234.7 71.0 %collective-permute-start.24 = (bf16[3,512,128]{2,1,0:T(8,128)(2,1)}, bf16[3,512,128]{2,1,0:T(8,128)(2,1)S(1)}, u32[]{:S(2)}, u32[]{:S(2)}) collective-permute-start(bf16[3,512,128]{2,1,0:T(8,128)(2,1)} %get-tuple-element.101), channel_id=1, source_target_pairs={{0,3},{1,0},{2,1},{3,2},{4,7},{5,4},{6,5},{7,6},{8,11},{9,8},{10,9... | collective-permute-start | bytes 1179656 | tf_op jit(solution)/shard_map/ppermute | solution.py:217
  242.4 65.3 %collective-permute-start.25 = (bf16[3,512,128]{2,1,0:T(8,128)(2,1)}, bf16[3,512,128]{2,1,0:T(8,128)(2,1)S(1)}, u32[]{:S(2)}, u32[]{:S(2)}) collective-permute-start(bf16[3,512,128]{2,1,0:T(8,128)(2,1)} %get-tuple-element.102), channel_id=1, source_target_pairs={{0,2},{1,3},{2,0},{3,1},{4,6},{5,7},{6,4},{7,5},{8,10},{9,11},{10,... | collective-permute-start | bytes 1179656 | tf_op jit(solution)/shard_map/ppermute | solution.py:217
  242.5 67.6 %collective-permute-start.26 = (bf16[3,512,128]{2,1,0:T(8,128)(2,1)}, bf16[3,512,128]{2,1,0:T(8,128)(2,1)}, u32[]{:S(2)}, u32[]{:S(2)}) collective-permute-start(bf16[3,512,128]{2,1,0:T(8,128)(2,1)} %get-tuple-element.103), channel_id=1, source_target_pairs={{0,1},{1,2},{2,3},{3,0},{4,5},{5,6},{6,7},{7,4},{8,9},{9,10},{10,1... | collective-permute-start | bytes 1179656 | tf_op jit(solution)/shard_map/ppermute | solution.py:217
  305.7 39.9 %collective-permute-start.22 = (bf16[3,512,128]{2,1,0:T(8,128)(2,1)}, bf16[3,512,128]{2,1,0:T(8,128)(2,1)S(1)}, u32[]{:S(2)}, u32[]{:S(2)}) collective-permute-start(bf16[3,512,128]{2,1,0:T(8,128)(2,1)} %get-tuple-element.98), channel_id=1, source_target_pairs={{0,2},{1,3},{2,0},{3,1},{4,6},{5,7},{6,4},{7,5},{8,10},{9,11},{10,... | collective-permute-start | bytes 1179656 | tf_op jit(solution)/shard_map/ppermute | solution.py:217
  305.7 39.9 %collective-permute-start.23 = (bf16[3,512,128]{2,1,0:T(8,128)(2,1)}, bf16[3,512,128]{2,1,0:T(8,128)(2,1)S(1)}, u32[]{:S(2)}, u32[]{:S(2)}) collective-permute-start(bf16[3,512,128]{2,1,0:T(8,128)(2,1)} %get-tuple-element.99), channel_id=1, source_target_pairs={{0,1},{1,2},{2,3},{3,0},{4,5},{5,6},{6,7},{7,4},{8,9},{9,10},{10,1... | collective-permute-start | bytes 1179656 | tf_op jit(solution)/shard_map/ppermute | solution.py:217
  307.7 41.8 %collective-permute-start.15 = (bf16[3,512,128]{2,1,0:T(8,128)(2,1)}, bf16[3,512,128]{2,1,0:T(8,128)(2,1)S(1)}, u32[]{:S(2)}, u32[]{:S(2)}) collective-permute-start(bf16[3,512,128]{2,1,0:T(8,128)(2,1)} %get-tuple-element.89), channel_id=1, source_target_pairs={{0,3},{1,0},{2,1},{3,2},{4,7},{5,4},{6,5},{7,6},{8,11},{9,8},{10,9... | collective-permute-start | bytes 1179656 | tf_op jit(solution)/shard_map/ppermute | solution.py:217
  310.1 56.5 %collective-permute-start.16 = (bf16[3,512,128]{2,1,0:T(8,128)(2,1)}, bf16[3,512,128]{2,1,0:T(8,128)(2,1)S(1)}, u32[]{:S(2)}, u32[]{:S(2)}) collective-permute-start(bf16[3,512,128]{2,1,0:T(8,128)(2,1)} %get-tuple-element.90), channel_id=1, source_target_pairs={{0,2},{1,3},{2,0},{3,1},{4,6},{5,7},{6,4},{7,5},{8,10},{9,11},{10,... | collective-permute-start | bytes 1179656 | tf_op jit(solution)/shard_map/ppermute | solution.py:217
  310.7 55.9 %collective-permute-start.17 = (bf16[3,512,128]{2,1,0:T(8,128)(2,1)}, bf16[3,512,128]{2,1,0:T(8,128)(2,1)S(1)}, u32[]{:S(2)}, u32[]{:S(2)}) collective-permute-start(bf16[3,512,128]{2,1,0:T(8,128)(2,1)} %get-tuple-element.91), channel_id=1, source_target_pairs={{0,1},{1,2},{2,3},{3,0},{4,5},{5,6},{6,7},{7,4},{8,9},{9,10},{10,1... | collective-permute-start | bytes 1179656 | tf_op jit(solution)/shard_map/ppermute | solution.py:217
  (29 other events, 567.9 us)
where the time goes:
time: 371 us
  starting transfers between devices  136 us (37%)
  Pallas kernels  115 us (31%)
  waiting for transfers between devices  46.5 us (13%)
  blocking collectives  32.4 us (9%)
  other arithmetic  20.5 us (6%)
  local copies, waits for them, and re-layouts  14.9 us (4%)
  matrix products  4.36 us (1%)
    ppermute x30, starting transfers between devices, shift(): return lax.ppermute(array, 'seq', ring)  129 us
    pallas_call x4, Pallas kernels, attend(): pl.pallas_call(functools.partial(attend_kernel, parts, rows, width, query...  90.5 us
    ppermute x30, waiting for transfers between devices, shift(): return lax.ppermute(array, 'seq', ring)  46.5 us
    unnamed x1, blocking collectives  23.3 us
    unnamed x1, other arithmetic  14.8 us
    pallas_call x4, Pallas kernels, unpack(): pl.pallas_call(functools.partial(unpack_kernel, parts), out_shape=[jax.Sh...  12.2 us
    pallas_call x4, Pallas kernels, pack(): pl.pallas_call(functools.partial(pack_kernel, parts), out_shape=[jax.Shap...  12.1 us
    unnamed x47, local copies, waits for them, and re-layouts  11.6 us
  transfers between devices with their start and end apart: 32, of which 4 were waited for; matrix products, arithmetic and copies ran while one was open for 10% of the time, Pallas kernels for 29%

commit v1 on v0

--- a/solution.py
+++ b/solution.py
@@ -252,11 +252,14 @@
         return arrays
 
     grad_parts = after(grad_parts, 0)
-    scale_parts = after(scale_parts, 1)
+    scale_parts = after(scale_parts, len(back) - 1)
     summed_grad = sum(grad_parts)
-    owner_grad = lax.all_to_all(summed_grad, "dp", split_axis=2, concat_axis=0, tiled=True)
+    shares = lax.axis_size("dp")
+    split_grad = summed_grad.reshape(samples * 2, shares, -1).transpose(1, 0, 2)
+    owner_grad = lax.all_to_all(split_grad, "dp", split_axis=0, concat_axis=0, tiled=True)
+    owner_grad = owner_grad.reshape(shares * samples, 2, -1)
     mod_scale = sum(scale_parts)
-    text_hidden, text_grad = after((text_hidden, text_grad), 1)
+    text_hidden, text_grad = after((text_hidden, text_grad), len(back) - 1)
     hidden = text_hidden.astype(jnp.float32)
     incoming = text_grad.astype(jnp.float32)
     centred = hidden - jnp.mean(hidden, axis=-1, keepdims=True)
@@ -275,7 +278,9 @@
     backward = jnp.einsum(
         "bkc,krc->br", owner_grad, mod_weight.astype(jnp.float32), precision=lax.Precision.HIGHEST
     )
-    summed_back = lax.psum_scatter(backward, "dp", scatter_dimension=0, tiled=True)
+    split_back = backward.reshape(shares, samples, -1)
+    split_back = lax.all_to_all(split_back, "dp", split_axis=0, concat_axis=0, tiled=True)
+    summed_back = jnp.sum(split_back, axis=0)
     sigma = jax.nn.sigmoid(cond_vec)
     cond_vec_grad = summed_back * sigma * (1.0 + cond_vec * (1.0 - sigma))
 

time: 371 us -> 363 us (0.978)
  waiting for transfers between devices: 46.5 us -> 78.9 us
  blocking collectives: 32.4 us -> 9.08 us
  other arithmetic: 20.5 us -> 5.75 us
  local copies, waits for them, and re-layouts: 14.9 us -> 4.69 us
  starting transfers between devices: 136 us -> 141 us
    ppermute x30, waiting for transfers between devices: 46.5 us -> 78.9 us  [shift(): return lax.ppermute(array, 'seq', ring)]
    unnamed x1 -> x0, blocking collectives: 23.3 us -> none
    unnamed x1 -> x0, other arithmetic: 14.8 us -> none
    unnamed x47 -> x23, local copies, waits for them, and re-layouts: 11.6 us -> 3.37 us
    all_to_all x1 -> x2, starting transfers between devices: 3.77 us -> 8.74 us  [the longest x1 4.71 us: per_device(): lax.all_to_all(split_back, 'dp', split_axis=0, concat_axis=0, tiled=True)]
  transfers between devices with their start and end apart: 32 -> 33, of which waited for: 4 -> 7; matrix products, arithmetic and copies ran while one was open for 10% -> 4% of each run, Pallas kernels for 29% -> 31%
where the time goes in v1:
time: 363 us; the launch traced here: 362 us
  starting transfers between devices  141 us (39%)
  Pallas kernels  118 us (33%)
  waiting for transfers between devices  78.9 us (22%)
  blocking collectives  9.08 us (3%)
  other arithmetic  5.75 us (2%)
  local copies, waits for them, and re-layouts  4.69 us (1%)
  matrix products  3.82 us (1%)
    ppermute x30, starting transfers between devices, shift(): return lax.ppermute(array, 'seq', ring)  129 us
    pallas_call x4, Pallas kernels, attend(): pl.pallas_call(functools.partial(attend_kernel, parts, rows, width, query...  93.4 us
    ppermute x30, waiting for transfers between devices, shift(): return lax.ppermute(array, 'seq', ring)  78.9 us
    pallas_call x4, Pallas kernels, unpack(): pl.pallas_call(functools.partial(unpack_kernel, parts), out_shape=[jax.Sh...  12.3 us
    pallas_call x4, Pallas kernels, pack(): pl.pallas_call(functools.partial(pack_kernel, parts), out_shape=[jax.Shap...  12.2 us
    all_gather x1, blocking collectives, per_device(): cond_all = lax.all_gather(cond_vec, 'dp', axis=0, tiled=True)  9.08 us
  transfers between devices with their start and end apart: 33, of which 7 were waited for; matrix products, arithmetic and copies ran while one was open for 4% of the time, Pallas kernels for 31%

profile of v1, /device:TPU:0, one launch (start us, length us, event | category | flops | bytes accessed | tf_op | source)
XLA Modules:
  0.0 362.3 jit_solution(14552889348946254260)
XLA Ops:
  0.6 3.1 pack.5
  3.7 4.1 %collective-permute-start.10 = (bf16[4,512,128]{2,1,0:T(8,128)(2,1)}, bf16[4,512,128]{2,1,0:T(8,128)(2,1)}, u32[]{:S(2)}, u32[]{:S(2)}) collective-permute-start(bf16[4,512,128]{2,1,0:T(8,128)(2,1)} %get-tuple-element.77), channel_id=1, source_target_pairs={{0,2},{1,3},{2,0},{3,1},{4,6},{5,7},{6,4},{7,5},{8,10},{9,11},{10,... | collective-permute-start | bytes 1572872 | tf_op jit(solution)/shard_map/ppermute | solution.py:217
  16.6 9.1 %all-gather = f32[8,1,768]{2,1,0:T(1,128)S(1)} all-gather(f32[1,1,768]{2,1,0:T(1,128)S(1)} %bitcast.122), channel_id=1, replica_groups=mesh['dp'=8,'seq'=4] {'dp'}, dimensions={0}, use_global_device_ids=true | all-gather | bytes 27648 | tf_op jit(solution)/shard_map/all_gather | solution.py:229
  27.1 3.3 all-to-all-start
  33.0 13.1 %collective-permute-start.5 = (bf16[4,512,128]{2,1,0:T(8,128)(2,1)}, bf16[4,512,128]{2,1,0:T(8,128)(2,1)}, u32[]{:S(2)}, u32[]{:S(2)}) collective-permute-start(bf16[4,512,128]{2,1,0:T(8,128)(2,1)} %get-tuple-element.66), channel_id=1, source_target_pairs={{0,3},{1,0},{2,1},{3,2},{4,7},{5,4},{6,5},{7,6},{8,11},{9,8},{10,9... | collective-permute-start | bytes 1572872 | tf_op jit(solution)/shard_map/ppermute | solution.py:217
  46.2 3.1 pack.7
  52.3 24.4 %collective-permute-start.6 = (f32[1,2,3072]{2,1,0:T(2,128)S(1)}, f32[1,2,3072]{2,1,0:T(2,128)S(1)}, u32[]{:S(2)}, u32[]{:S(2)}) collective-permute-start(f32[1,2,3072]{2,1,0:T(2,128)S(1)} %pad_maximum_fusion), channel_id=1, source_target_pairs={{0,2},{1,3},{2,0},{3,1},{4,6},{5,7},{6,4},{7,5},{8,10},{9,11},{10,... | collective-permute-start | bytes 73736 | tf_op jit(solution)/shard_map/ppermute | solution.py:217
  77.7 23.4 %attend.5 = (bf16[3,512,128]{2,1,0:T(8,128)(2,1)}, bf16[3,512,128]{2,1,0:T(8,128)(2,1)}, bf16[3,512,128]{2,1,0:T(8,128)(2,1)}, bf16[3,512,128]{2,1,0:T(8,128)(2,1)}) custom-call(bf16[4,512,128]{2,1,0:T(8,128)(2,1)} %get-tuple-element.75.refs_0_, bf16[4,512,128]{2,1,0:T(8,128)(2,1)} %collective-permute-done.9.refs_1_, ...), custom_call_target="tpu_custom_call" | custom-call | flops 5368709120 | bytes 3670016 | tf_op jit(solution)/shard_map/attend/pallas_call | solution.py:107
  108.7 23.4 %attend.4 = (bf16[3,512,128]{2,1,0:T(8,128)(2,1)}, bf16[3,512,128]{2,1,0:T(8,128)(2,1)}, bf16[3,512,128]{2,1,0:T(8,128)(2,1)}, bf16[3,512,128]{2,1,0:T(8,128)(2,1)}) custom-call(bf16[4,512,128]{2,1,0:T(8,128)(2,1)} %get-tuple-element.63.refs_0_, bf16[4,512,128]{2,1,0:T(8,128)(2,1)} %copy-done.10, bf16[4,512,128]{2,1,0:T(8,128)(2,1)} %collective-permute-done.4.refs_2_, ...), custom_call_target="tpu_custom_call" | custom-call | flops 5368709120 | bytes 3670016 | tf_op jit(solution)/shard_map/attend/pallas_call | solution.py:107
  138.6 4.0 %all-to-all-start.1 = ((f32[8,2,384]{2,1,0:T(2,128)}), f32[8,2,384]{2,1,0:T(2,128)}, u32[]{:S(2)}, u32[]{:S(2)}) async-start(f32[8,2,384]{2,1,0:T(2,128)} %bitcast.13), calls=%async_computation.1 | async-start | bytes 49152 | tf_op jit(solution)/shard_map/all_to_all | solution.py:259
  143.8 5.3 %collective-permute-done.21.refs_1_ = bf16[4,512,128]{2,1,0:T(8,128)(2,1)} collective-permute-done((bf16[4,512,128]{2,1,0:T(8,128)(2,1)}, bf16[4,512,128]{2,1,0:T(8,128)(2,1)}, u32[]{:S(2)}, u32[]{:S(2)}) %collective-permute-start.21) | collective-permute-done | bytes 524320 | tf_op jit(solution)/shard_map/ppermute | solution.py:217
  149.2 22.4 %collective-permute-done.22.refs_2_ = bf16[4,512,128]{2,1,0:T(8,128)(2,1)} collective-permute-done((bf16[4,512,128]{2,1,0:T(8,128)(2,1)}, bf16[4,512,128]{2,1,0:T(8,128)(2,1)}, u32[]{:S(2)}, u32[]{:S(2)}) %collective-permute-start.22) | collective-permute-done | bytes 524320 | tf_op jit(solution)/shard_map/ppermute | solution.py:217
  171.6 42.1 %collective-permute-start.27 = (bf16[3,512,128]{2,1,0:T(8,128)(2,1)}, bf16[3,512,128]{2,1,0:T(8,128)(2,1)}, u32[]{:S(2)}, u32[]{:S(2)}) collective-permute-start(bf16[3,512,128]{2,1,0:T(8,128)(2,1)} %get-tuple-element.105), channel_id=1, source_target_pairs={{0,3},{1,0},{2,1},{3,2},{4,7},{5,4},{6,5},{7,6},{8,11},{9,8},{10,9... | collective-permute-start | bytes 1179656 | tf_op jit(solution)/shard_map/ppermute | solution.py:217
  213.7 23.3 %attend.7 = (bf16[3,512,128]{2,1,0:T(8,128)(2,1)}, bf16[3,512,128]{2,1,0:T(8,128)(2,1)}, bf16[3,512,128]{2,1,0:T(8,128)(2,1)}, bf16[3,512,128]{2,1,0:T(8,128)(2,1)}) custom-call(bf16[4,512,128]{2,1,0:T(8,128)(2,1)} %get-tuple-element.96.refs_0_, bf16[4,512,128]{2,1,0:T(8,128)(2,1)} %collective-permute-done.21.refs_1_, ...), custom_call_target="tpu_custom_call" | custom-call | flops 5368709120 | bytes 3670016 | tf_op jit(solution)/shard_map/attend/pallas_call | solution.py:107
  237.5 7.8 %collective-permute-start.24 = (bf16[3,512,128]{2,1,0:T(8,128)(2,1)}, bf16[3,512,128]{2,1,0:T(8,128)(2,1)S(1)}, u32[]{:S(2)}, u32[]{:S(2)}) collective-permute-start(bf16[3,512,128]{2,1,0:T(8,128)(2,1)} %get-tuple-element.101), channel_id=1, source_target_pairs={{0,3},{1,0},{2,1},{3,2},{4,7},{5,4},{6,5},{7,6},{8,11},{9,8},{10,9... | collective-permute-start | bytes 1179656 | tf_op jit(solution)/shard_map/ppermute | solution.py:217
  245.4 23.3 %attend.6 = (bf16[3,512,128]{2,1,0:T(8,128)(2,1)}, bf16[3,512,128]{2,1,0:T(8,128)(2,1)}, bf16[3,512,128]{2,1,0:T(8,128)(2,1)}, bf16[3,512,128]{2,1,0:T(8,128)(2,1)}) custom-call(bf16[4,512,128]{2,1,0:T(8,128)(2,1)} %get-tuple-element.88.refs_0_, bf16[4,512,128]{2,1,0:T(8,128)(2,1)} %collective-permute-done.15.refs_1_, ...), custom_call_target="tpu_custom_call" | custom-call | flops 5368709120 | bytes 3670016 | tf_op jit(solution)/shard_map/attend/pallas_call | solution.py:107
  276.5 4.7 %all-to-all-start.2 = ((f32[8,1,768]{2,1,0:T(1,128)}), f32[8,1,768]{2,1,0:T(1,128)}, u32[]{:S(2)}, u32[]{:S(2)}) async-start(f32[8,1,768]{2,1,0:T(1,128)} %copy.27), calls=%async_computation.2 | async-start | bytes 49152 | tf_op jit(solution)/shard_map/all_to_all | solution.py:282
  281.2 4.6 %collective-permute-start.19 = (bf16[3,512,128]{2,1,0:T(8,128)(2,1)}, bf16[3,512,128]{2,1,0:T(8,128)(2,1)}, u32[]{:S(2)}, u32[]{:S(2)}) collective-permute-start(bf16[3,512,128]{2,1,0:T(8,128)(2,1)} %get-tuple-element.94), channel_id=1, source_target_pairs={{0,2},{1,3},{2,0},{3,1},{4,6},{5,7},{6,4},{7,5},{8,10},{9,11},{10,... | collective-permute-start | bytes 1179656 | tf_op jit(solution)/shard_map/ppermute | solution.py:217
  285.8 23.6 %collective-permute-done.25.refs_3_ = bf16[3,512,128]{2,1,0:T(8,128)(2,1)S(1)} collective-permute-done((bf16[3,512,128]{2,1,0:T(8,128)(2,1)}, bf16[3,512,128]{2,1,0:T(8,128)(2,1)S(1)}, u32[]{:S(2)}, u32[]{:S(2)}) %collective-permute-start.25) | collective-permute-done | bytes 393248 | tf_op jit(solution)/shard_map/ppermute | solution.py:217
  311.1 9.9 %collective-permute-start.14 = (bf16[3,512,128]{2,1,0:T(8,128)(2,1)}, bf16[3,512,128]{2,1,0:T(8,128)(2,1)}, u32[]{:S(2)}, u32[]{:S(2)}) collective-permute-start(bf16[3,512,128]{2,1,0:T(8,128)(2,1)} %get-tuple-element.87), channel_id=1, source_target_pairs={{0,1},{1,2},{2,3},{3,0},{4,5},{5,6},{6,7},{7,4},{8,9},{9,10},{10,1... | collective-permute-start | bytes 1179656 | tf_op jit(solution)/shard_map/ppermute | solution.py:217
  329.3 3.1 unpack.5
  332.4 10.8 %collective-permute-done.19.refs_3_ = bf16[3,512,128]{2,1,0:T(8,128)(2,1)} collective-permute-done((bf16[3,512,128]{2,1,0:T(8,128)(2,1)}, bf16[3,512,128]{2,1,0:T(8,128)(2,1)}, u32[]{:S(2)}, u32[]{:S(2)}) %collective-permute-start.19) | collective-permute-done | bytes 393248 | tf_op jit(solution)/shard_map/ppermute | solution.py:217
  346.3 12.9 %collective-permute-done.13.refs_3_ = bf16[3,512,128]{2,1,0:T(8,128)(2,1)} collective-permute-done((bf16[3,512,128]{2,1,0:T(8,128)(2,1)}, bf16[3,512,128]{2,1,0:T(8,128)(2,1)}, u32[]{:S(2)}, u32[]{:S(2)}) %collective-permute-start.13) | collective-permute-done | bytes 393248 | tf_op jit(solution)/shard_map/ppermute | solution.py:217
  359.2 3.1 unpack.7
  (100 shorter events, 53.7 us)
Async XLA Ops:
  7.8 44.5 %collective-permute-start.11 = (bf16[4,512,128]{2,1,0:T(8,128)(2,1)}, bf16[4,512,128]{2,1,0:T(8,128)(2,1)}, u32[]{:S(2)}, u32[]{:S(2)}) collective-permute-start(bf16[4,512,128]{2,1,0:T(8,128)(2,1)} %get-tuple-element.78), channel_id=1, source_target_pairs={{0,3},{1,0},{2,1},{3,2},{4,7},{5,4},{6,5},{7,6},{8,11},{9,8},{10,9... | collective-permute-start | bytes 1572872 | tf_op jit(solution)/shard_map/ppermute | solution.py:217
  9.1 67.5 %collective-permute-start.9 = (bf16[4,512,128]{2,1,0:T(8,128)(2,1)}, bf16[4,512,128]{2,1,0:T(8,128)(2,1)}, u32[]{:S(2)}, u32[]{:S(2)}) collective-permute-start(bf16[4,512,128]{2,1,0:T(8,128)(2,1)} %get-tuple-element.76), channel_id=1, source_target_pairs={{0,1},{1,2},{2,3},{3,0},{4,5},{5,6},{6,7},{7,4},{8,9},{9,10},{10,1... | collective-permute-start | bytes 1572872 | tf_op jit(solution)/shard_map/ppermute | solution.py:217
  12.8 91.1 %collective-permute-start.3 = (bf16[4,512,128]{2,1,0:T(8,128)(2,1)}, bf16[4,512,128]{2,1,0:T(8,128)(2,1)S(1)}, u32[]{:S(2)}, u32[]{:S(2)}) collective-permute-start(bf16[4,512,128]{2,1,0:T(8,128)(2,1)} %get-tuple-element.64), channel_id=1, source_target_pairs={{0,1},{1,2},{2,3},{3,0},{4,5},{5,6},{6,7},{7,4},{8,9},{9,10},{10,1... | collective-permute-start | bytes 1572872 | tf_op jit(solution)/shard_map/ppermute | solution.py:217
  14.5 90.4 %collective-permute-start.4 = (bf16[4,512,128]{2,1,0:T(8,128)(2,1)}, bf16[4,512,128]{2,1,0:T(8,128)(2,1)}, u32[]{:S(2)}, u32[]{:S(2)}) collective-permute-start(bf16[4,512,128]{2,1,0:T(8,128)(2,1)} %get-tuple-element.65), channel_id=1, source_target_pairs={{0,2},{1,3},{2,0},{3,1},{4,6},{5,7},{6,4},{7,5},{8,10},{9,11},{10,... | collective-permute-start | bytes 1572872 | tf_op jit(solution)/shard_map/ppermute | solution.py:217
  27.1 76.8 %all-to-all-start = ((f32[8,1,384]{2,1,0:T(1,128)}), f32[8,1,384]{2,1,0:T(1,128)S(1)}, u32[]{:S(2)}, u32[]{:S(2)}) async-start(f32[8,1,384]{2,1,0:T(1,128)} %copy.24), calls=%async_computation | async-start | bytes 24576 | tf_op jit(solution)/shard_map/all_to_all | solution.py:232
  33.0 73.8 %collective-permute-start.5 = (bf16[4,512,128]{2,1,0:T(8,128)(2,1)}, bf16[4,512,128]{2,1,0:T(8,128)(2,1)}, u32[]{:S(2)}, u32[]{:S(2)}) collective-permute-start(bf16[4,512,128]{2,1,0:T(8,128)(2,1)} %get-tuple-element.66), channel_id=1, source_target_pairs={{0,3},{1,0},{2,1},{3,2},{4,7},{5,4},{6,5},{7,6},{8,11},{9,8},{10,9... | collective-permute-start | bytes 1572872 | tf_op jit(solution)/shard_map/ppermute | solution.py:217
  52.3 48.8 %collective-permute-start.6 = (f32[1,2,3072]{2,1,0:T(2,128)S(1)}, f32[1,2,3072]{2,1,0:T(2,128)S(1)}, u32[]{:S(2)}, u32[]{:S(2)}) collective-permute-start(f32[1,2,3072]{2,1,0:T(2,128)S(1)} %pad_maximum_fusion), channel_id=1, source_target_pairs={{0,2},{1,3},{2,0},{3,1},{4,6},{5,7},{6,4},{7,5},{8,10},{9,11},{10,... | collective-permute-start | bytes 73736 | tf_op jit(solution)/shard_map/ppermute | solution.py:217
  76.6 55.4 %collective-permute-start.7 = (f32[1,2,3072]{2,1,0:T(2,128)S(1)}, f32[1,2,3072]{2,1,0:T(2,128)S(1)}, u32[]{:S(2)}, u32[]{:S(2)}) collective-permute-start(f32[1,2,3072]{2,1,0:T(2,128)S(1)} %pad_maximum_fusion), channel_id=1, source_target_pairs={{0,1},{1,2},{2,3},{3,0},{4,5},{5,6},{6,7},{7,4},{8,9},{9,10},{10,1... | collective-permute-start | bytes 73736 | tf_op jit(solution)/shard_map/ppermute | solution.py:217
  133.1 80.5 %collective-permute-start.23 = (bf16[4,512,128]{2,1,0:T(8,128)(2,1)}, bf16[4,512,128]{2,1,0:T(8,128)(2,1)}, u32[]{:S(2)}, u32[]{:S(2)}) collective-permute-start(bf16[4,512,128]{2,1,0:T(8,128)(2,1)} %get-tuple-element.99), channel_id=1, source_target_pairs={{0,3},{1,0},{2,1},{3,2},{4,7},{5,4},{6,5},{7,6},{8,11},{9,8},{10,9... | collective-permute-start | bytes 1572872 | tf_op jit(solution)/shard_map/ppermute | solution.py:217
  136.0 101.0 %collective-permute-start.15 = (bf16[4,512,128]{2,1,0:T(8,128)(2,1)}, bf16[4,512,128]{2,1,0:T(8,128)(2,1)}, u32[]{:S(2)}, u32[]{:S(2)}) collective-permute-start(bf16[4,512,128]{2,1,0:T(8,128)(2,1)} %get-tuple-element.89), channel_id=1, source_target_pairs={{0,1},{1,2},{2,3},{3,0},{4,5},{5,6},{6,7},{7,4},{8,9},{9,10},{10,1... | collective-permute-start | bytes 1572872 | tf_op jit(solution)/shard_map/ppermute | solution.py:217
  136.5 101.0 %collective-permute-start.16 = (bf16[4,512,128]{2,1,0:T(8,128)(2,1)S(1)}, bf16[4,512,128]{2,1,0:T(8,128)(2,1)}, u32[]{:S(2)}, u32[]{:S(2)}) collective-permute-start(bf16[4,512,128]{2,1,0:T(8,128)(2,1)S(1)} %copy-done.9), channel_id=1, source_target_pairs={{0,2},{1,3},{2,0},{3,1},{4,6},{5,7},{6,4},{7,5},{8,10},{9,11},{10,... | collective-permute-start | bytes 1572872 | tf_op jit(solution)/shard_map/ppermute | solution.py:217
  138.6 135.4 %all-to-all-start.1 = ((f32[8,2,384]{2,1,0:T(2,128)}), f32[8,2,384]{2,1,0:T(2,128)}, u32[]{:S(2)}, u32[]{:S(2)}) async-start(f32[8,2,384]{2,1,0:T(2,128)} %bitcast.13), calls=%async_computation.1 | async-start | bytes 49152 | tf_op jit(solution)/shard_map/all_to_all | solution.py:259
  149.1 96.3 %collective-permute-start.17 = (bf16[4,512,128]{2,1,0:T(8,128)(2,1)S(1)}, bf16[4,512,128]{2,1,0:T(8,128)(2,1)}, u32[]{:S(2)}, u32[]{:S(2)}) collective-permute-start(bf16[4,512,128]{2,1,0:T(8,128)(2,1)S(1)} %copy-done.8), channel_id=1, source_target_pairs={{0,3},{1,0},{2,1},{3,2},{4,7},{5,4},{6,5},{7,6},{8,11},{9,8},{10,9... | collective-permute-start | bytes 1572872 | tf_op jit(solution)/shard_map/ppermute | solution.py:217
  171.6 97.1 %collective-permute-start.27 = (bf16[3,512,128]{2,1,0:T(8,128)(2,1)}, bf16[3,512,128]{2,1,0:T(8,128)(2,1)}, u32[]{:S(2)}, u32[]{:S(2)}) collective-permute-start(bf16[3,512,128]{2,1,0:T(8,128)(2,1)} %get-tuple-element.105), channel_id=1, source_target_pairs={{0,3},{1,0},{2,1},{3,2},{4,7},{5,4},{6,5},{7,6},{8,11},{9,8},{10,9... | collective-permute-start | bytes 1179656 | tf_op jit(solution)/shard_map/ppermute | solution.py:217
  213.7 57.9 %collective-permute-start.28 = (bf16[3,512,128]{2,1,0:T(8,128)(2,1)}, bf16[3,512,128]{2,1,0:T(8,128)(2,1)}, u32[]{:S(2)}, u32[]{:S(2)}) collective-permute-start(bf16[3,512,128]{2,1,0:T(8,128)(2,1)} %get-tuple-element.106), channel_id=1, source_target_pairs={{0,2},{1,3},{2,0},{3,1},{4,6},{5,7},{6,4},{7,5},{8,10},{9,11},{10,... | collective-permute-start | bytes 1179656 | tf_op jit(solution)/shard_map/ppermute | solution.py:217
  237.0 44.2 %collective-permute-start.29 = (bf16[3,512,128]{2,1,0:T(8,128)(2,1)}, bf16[3,512,128]{2,1,0:T(8,128)(2,1)}, u32[]{:S(2)}, u32[]{:S(2)}) collective-permute-start(bf16[3,512,128]{2,1,0:T(8,128)(2,1)} %get-tuple-element.107), channel_id=1, source_target_pairs={{0,1},{1,2},{2,3},{3,0},{4,5},{5,6},{6,7},{7,4},{8,9},{9,10},{10,1... | collective-permute-start | bytes 1179656 | tf_op jit(solution)/shard_map/ppermute | solution.py:217
  237.5 48.3 %collective-permute-start.24 = (bf16[3,512,128]{2,1,0:T(8,128)(2,1)}, bf16[3,512,128]{2,1,0:T(8,128)(2,1)S(1)}, u32[]{:S(2)}, u32[]{:S(2)}) collective-permute-start(bf16[3,512,128]{2,1,0:T(8,128)(2,1)} %get-tuple-element.101), channel_id=1, source_target_pairs={{0,3},{1,0},{2,1},{3,2},{4,7},{5,4},{6,5},{7,6},{8,11},{9,8},{10,9... | collective-permute-start | bytes 1179656 | tf_op jit(solution)/shard_map/ppermute | solution.py:217
  245.4 64.1 %collective-permute-start.25 = (bf16[3,512,128]{2,1,0:T(8,128)(2,1)}, bf16[3,512,128]{2,1,0:T(8,128)(2,1)S(1)}, u32[]{:S(2)}, u32[]{:S(2)}) collective-permute-start(bf16[3,512,128]{2,1,0:T(8,128)(2,1)} %get-tuple-element.102), channel_id=1, source_target_pairs={{0,2},{1,3},{2,0},{3,1},{4,6},{5,7},{6,4},{7,5},{8,10},{9,11},{10,... | collective-permute-start | bytes 1179656 | tf_op jit(solution)/shard_map/ppermute | solution.py:217
  268.7 40.7 %collective-permute-start.26 = (bf16[3,512,128]{2,1,0:T(8,128)(2,1)}, bf16[3,512,128]{2,1,0:T(8,128)(2,1)}, u32[]{:S(2)}, u32[]{:S(2)}) collective-permute-start(bf16[3,512,128]{2,1,0:T(8,128)(2,1)} %get-tuple-element.103), channel_id=1, source_target_pairs={{0,1},{1,2},{2,3},{3,0},{4,5},{5,6},{6,7},{7,4},{8,9},{9,10},{10,1... | collective-permute-start | bytes 1179656 | tf_op jit(solution)/shard_map/ppermute | solution.py:217
  276.5 48.4 %all-to-all-start.2 = ((f32[8,1,768]{2,1,0:T(1,128)}), f32[8,1,768]{2,1,0:T(1,128)}, u32[]{:S(2)}, u32[]{:S(2)}) async-start(f32[8,1,768]{2,1,0:T(1,128)} %copy.27), calls=%async_computation.2 | async-start | bytes 49152 | tf_op jit(solution)/shard_map/all_to_all | solution.py:282
  281.2 62.0 %collective-permute-start.19 = (bf16[3,512,128]{2,1,0:T(8,128)(2,1)}, bf16[3,512,128]{2,1,0:T(8,128)(2,1)}, u32[]{:S(2)}, u32[]{:S(2)}) collective-permute-start(bf16[3,512,128]{2,1,0:T(8,128)(2,1)} %get-tuple-element.94), channel_id=1, source_target_pairs={{0,2},{1,3},{2,0},{3,1},{4,6},{5,7},{6,4},{7,5},{8,10},{9,11},{10,... | collective-permute-start | bytes 1179656 | tf_op jit(solution)/shard_map/ppermute | solution.py:217
  285.8 57.4 %collective-permute-start.20 = (bf16[3,512,128]{2,1,0:T(8,128)(2,1)}, bf16[3,512,128]{2,1,0:T(8,128)(2,1)}, u32[]{:S(2)}, u32[]{:S(2)}) collective-permute-start(bf16[3,512,128]{2,1,0:T(8,128)(2,1)} %get-tuple-element.95), channel_id=1, source_target_pairs={{0,1},{1,2},{2,3},{3,0},{4,5},{5,6},{6,7},{7,4},{8,9},{9,10},{10,1... | collective-permute-start | bytes 1179656 | tf_op jit(solution)/shard_map/ppermute | solution.py:217
  309.4 49.7 %collective-permute-start.13 = (bf16[3,512,128]{2,1,0:T(8,128)(2,1)}, bf16[3,512,128]{2,1,0:T(8,128)(2,1)}, u32[]{:S(2)}, u32[]{:S(2)}) collective-permute-start(bf16[3,512,128]{2,1,0:T(8,128)(2,1)} %get-tuple-element.86), channel_id=1, source_target_pairs={{0,2},{1,3},{2,0},{3,1},{4,6},{5,7},{6,4},{7,5},{8,10},{9,11},{10,... | collective-permute-start | bytes 1179656 | tf_op jit(solution)/shard_map/ppermute | solution.py:217
  311.1 48.1 %collective-permute-start.14 = (bf16[3,512,128]{2,1,0:T(8,128)(2,1)}, bf16[3,512,128]{2,1,0:T(8,128)(2,1)}, u32[]{:S(2)}, u32[]{:S(2)}) collective-permute-start(bf16[3,512,128]{2,1,0:T(8,128)(2,1)} %get-tuple-element.87), channel_id=1, source_target_pairs={{0,1},{1,2},{2,3},{3,0},{4,5},{5,6},{6,7},{7,4},{8,9},{9,10},{10,1... | collective-permute-start | bytes 1179656 | tf_op jit(solution)/shard_map/ppermute | solution.py:217
  (20 other events, 449.5 us)
